TPU v7x, 128 devices: a whole 4x4x4 slice. The times are simulated.
128 devices in a mesh: sx: 8 (over y, core), sy: 16 (over x, z).
Axes of the slice: x: 4, y: 4, z: 4, core: 2. Of those that a mesh axis runs over, the one named last changes fastest.
Arguments:
- loads: float32 [8, 16, 1536, 256], P('sx', 'sy')
- schur_flex: float32 [8, 16, 1536, 1536], P('sx', 'sy'), as said below
- dirichlet: float32 [8, 16, 1536, 1536], P('sx', 'sy'), as said below
- coupling: float32 [8, 16, 16, 1536], P('sx', 'sy'), may hold values from -0.3125 to 0.3125
- corner_index: int32 [8, 16, 16], P('sx', 'sy'), may hold values from 0 to 512, as said below
- face_lists: int32 [8, 16, 4, 384], P('sx', 'sy'), may hold values from 0 to 383, as said below
- coarse_inverse: float32 [512, 512], P(('sx', 'sy')), as said below
Outputs:
- multipliers: float32 [8, 16, 1536, 256], P('sx', 'sy')
- residual: float32 [8, 16, 1536, 256], P('sx', 'sy')
Inputs may be any that keep to these rules, and one draw needn't show every extreme that they name: `corner_index`: each subdomain lists 4 coarse dofs for each of its four corners; 512 marks a corner on the clamped edges of the panel, which has no coarse dof; every coarse dof below 512 is named by some subdomain. `face_lists`: each face's list is a permutation of the 384 dofs of the facing face; the facing lists of two neighbouring subdomains are inverse permutations. `schur_flex`: symmetric positive definite for every subdomain. `dirichlet`: symmetric positive definite for every subdomain. `coarse_inverse`: symmetric positive definite.
All inputs are finite; a program needn't handle non-finite values.
Results may differ from a plain program's by a relative error of at most 0.00017.
Values sent between devices are 32-bit elements; how exact they have to be, the bound alone decides.
A program may use at most 128 MiB of HBM per device.

v0:
```python
import jax
import jax.numpy as jnp
from jax import lax
from jax.sharding import PartitionSpec as P

HIGH = lax.Precision.HIGH
HIGHEST = lax.Precision.HIGHEST


def shifted(block, axis, distance):
    devices = range(lax.axis_size(axis))
    route = [(i - distance, i) for i in devices if i - distance in devices]
    return lax.ppermute(block, axis, route)


def facing(faces):
    return (
        shifted(faces[1], "sx", 1),
        shifted(faces[0], "sx", -1),
        shifted(faces[3], "sy", 1),
        shifted(faces[2], "sy", -1),
    )


def jump(field, match):
    size = field.shape[0] // 4
    faces = [field[f * size : (f + 1) * size] for f in range(4)]
    received = facing(faces)
    return jnp.concatenate(
        [faces[f] - jnp.dot(match[f], received[f], precision=HIGHEST) for f in range(4)], axis=0
    )


def inner(first, second):
    return jnp.sum(first * second, axis=0)


def shards(loads, schur_flex, dirichlet, coupling, corner_index, face_lists, coarse_inverse):
    flex_mat = schur_flex[0, 0]
    prec_mat = dirichlet[0, 0]
    coupling_mat = coupling[0, 0]
    corners = corner_index[0, 0]
    face_index = face_lists[0, 0]
    ncoarse = coarse_inverse.shape[1]
    ncl = corners.shape[0]
    size = face_index.shape[1]
    sx = lax.axis_index("sx")
    sy = lax.axis_index("sy")
    inside = jnp.stack([sx > 0, sx < lax.axis_size("sx") - 1, sy > 0, sy < lax.axis_size("sy") - 1])
    scale = jnp.repeat(1.0 + inside.astype(jnp.float32), size)[:, None]
    match = (face_index[:, :, None] == jnp.arange(size, dtype=jnp.int32)[None, None, :]).astype(
        jnp.float32
    )
    inverse = lax.all_gather(coarse_inverse, ("sx", "sy"), axis=0, tiled=True)
    slots = jnp.concatenate([corners, jnp.arange(ncoarse + 1, ncoarse + 4, dtype=jnp.int32)])
    place = (slots[None, :] == jnp.arange(ncoarse + 8, dtype=jnp.int32)[:, None]).astype(
        jnp.float32
    )
    coarse_ids = jnp.arange(ncoarse, dtype=jnp.float32)[None, :]
    own = corners.astype(jnp.float32)
    parts = [coupling_mat[:, f * size : (f + 1) * size].T for f in range(4)]
    tagged = [jnp.concatenate([part, jnp.broadcast_to(own, (8, ncl))], axis=0) for part in parts]
    pick = (own[:, None] == coarse_ids).astype(jnp.float32)
    columns = []
    for f, got in enumerate(facing(tagged)):
        their_pick = (got[size][:, None] == coarse_ids).astype(jnp.float32)
        theirs = jnp.dot(match[f], got[:size], precision=HIGHEST)
        columns.append(
            jnp.dot(parts[f], pick, precision=HIGHEST)
            - jnp.dot(theirs, their_pick, precision=HIGHEST)
        )
    coupling_jump = jnp.concatenate(columns, axis=0)

    def reduced(local_load, *rows):
        rows = list(rows) + [jnp.zeros_like(rows[0])] * (3 - len(rows))
        block = jnp.concatenate([local_load] + [row[None] for row in rows], axis=0)
        total = lax.psum(jnp.dot(place, block, precision=HIGHEST), ("sx", "sy"))
        return (total[:ncoarse], total[ncoarse + 1], total[ncoarse + 2], total[ncoarse + 3])

    def coarse(rhs):
        sol = jnp.dot(inverse, rhs, precision=HIGHEST)
        return (jnp.dot(coupling_jump, sol, precision=HIGHEST), inner(rhs, sol))

    def precondition(residual):
        spread = scale * residual
        applied = jnp.dot(prec_mat, spread, precision=HIGH)
        return (0.5 * jump(applied, match), 0.5 * inner(spread, applied))

    def flexible(direction):
        spread = scale * direction
        return (
            spread,
            jnp.dot(flex_mat, spread, precision=HIGH),
            jnp.dot(coupling_mat, spread, precision=HIGH),
        )

    residual = jump(loads[0, 0], match)
    direction, dot_part = precondition(residual)
    spread, flexed, load = flexible(direction)
    rhs, res_dot, energy, _ = reduced(load, dot_part, inner(spread, flexed))
    image = jump(flexed, match)
    correction, coarse_energy = coarse(rhs)
    step = res_dot / (energy + coarse_energy)
    residual = residual - step * (image + correction)
    multipliers = step * direction
    precond, dot_part = precondition(residual)
    spread, new_flexed, load = flexible(precond)
    new_rhs, new_dot, new_energy, cross = reduced(
        load, dot_part, inner(spread, new_flexed), inner(spread, flexed)
    )
    new_image = jump(new_flexed, match)
    beta = new_dot / res_dot
    rhs = new_rhs + beta * rhs
    energy = new_energy + beta * (2.0 * cross + beta * energy)
    correction, coarse_energy = coarse(rhs)
    step = new_dot / (energy + coarse_energy)
    multipliers = multipliers + step * (precond + beta * direction)
    residual = residual - step * (new_image + beta * image + correction)
    return (multipliers[None, None], residual[None, None])


def solution(mesh):
    return jax.shard_map(
        shards,
        mesh=mesh,
        in_specs=(
            P("sx", "sy", None, None),
            P("sx", "sy", None, None),
            P("sx", "sy", None, None),
            P("sx", "sy", None, None),
            P("sx", "sy", None),
            P("sx", "sy", None, None),
            P(("sx", "sy"), None),
        ),
        out_specs=(P("sx", "sy", None, None), P("sx", "sy", None, None)),
        check_vma=False,
    )
```

profile of v0, /device:TPU:1, one launch (start us, length us, event | category | flops | bytes accessed | tf_op | source)
XLA Modules:
  0.0 480.3 jit_solution(9736556489605518894)
XLA Ops:
  9.5 4.6 collective-permute-start.12
  16.0 3.5 collective-permute-start.14
  23.5 3.9 collective-permute-start
  36.4 4.3 collective-permute-start.2
  49.7 5.8 %collective-permute-done.3 = f32[384,256]{1,0:T(8,128)S(1)} collective-permute-done((f32[384,256]{1,0:T(8,128)S(1)}, f32[384,256]{1,0:T(8,128)S(1)}, u32[]{:S(2)}, u32[]{:S(2)}) %collective-permute-start.3) | collective-permute-done | bytes 393248 | tf_op jit(solution)/shard_map/ppermute | solution.py:13
  56.1 4.1 multiply_reduce_fusion.4
  60.4 4.6 collective-permute-start.4
  66.4 3.4 collective-permute-start.6
  74.2 4.1 collective-permute-done.6
  78.8 3.3 collective-permute-done.7
  83.3 4.2 multiply_reduce_fusion.3
  88.4 4.1 collective-permute-start.8
  92.5 5.6 %collective-permute-start.10 = (f32[384,256]{1,0:T(8,128)}, f32[384,256]{1,0:T(8,128)}, u32[]{:S(2)}, u32[]{:S(2)}) collective-permute-start(f32[384,256]{1,0:T(8,128)} %get-tuple-element.13), channel_id=1, source_target_pairs={{0,1},{1,2},{2,3},{3,4},{4,5},{5,6},{6,7},{7,8},{8,9},{9,10},{10,1... | collective-permute-start | bytes 1179656 | tf_op jit(solution)/shard_map/ppermute | solution.py:13
  116.8 134.1 %all-reduce.3.cloned.1.call-done = f32[520,256]{1,0:T(8,128)} async-done(((f32[520,256]{1,0:T(8,128)}), f32[520,256]{1,0:T(8,128)}) %all-reduce.3.cloned.1.call-update) | async-done | bytes 532496 | tf_op jit(solution)/shard_map/psum | solution.py:77
  251.0 3.7 fusion.36
  258.8 5.7 %fusion.9 = f32[1536,256]{1,0:T(8,128)S(1)} fusion(f32[256,512]{1,0:T(8,128)} %fusion.36, f32[384,512]{1,0:T(8,128)} %convolution_subtract_fusion, f32[384,512]{1,0:T(8,128)} %convolution_subtract_fusion.1, f32[384,512]{1,0:T(8,128)} %convolution_subtract_fusion.2, f32[384,512]{1,0:T(8,128)} %convolution_subtract_fusion.3, ...), kind=kOutput, calls=%fused_computation.11 | convolution fusion | flops 2421817344 | bytes 8389632 | tf_op jit(solution)/shard_map/dot_general | solution.py:82
  264.6 7.4 %multiply_reduce_fusion.2 = (f32[256]{0:T(256)S(1)}, f32[1536,256]{1,0:T(8,128)S(1)}) fusion(f32[1536,256]{1,0:T(8,128)S(1)} %fusion.9, f32[1536]{0:T(1024)S(1)} %mul.194, f32[1,1,1536,1536]{3,2,1,0:T(8,128)} %param.9), kind=kOutput, calls=%fused_computation.34 | convolution fusion | flops 3625451264 | bytes 12590080 | tf_op jit(solution)/shard_map/dot_general | solution.py:86
  281.6 4.1 collective-permute-done.18
  290.7 5.8 %multiply_reduce_fusion.1 = (f32[256]{0:T(256)S(1)}, f32[256]{0:T(256)S(1)}, f32[1536,256]{1,0:T(8,128)}) fusion(f32[1536]{0:T(1024)S(1)} %broadcast_multiply_fusion, f32[384,256]{1,0:T(8,128)S(1)} %convolution_subtract_fusion.8, f32[384,256]{1,0:T(8,128)S(1)} %convolution_subtract_fusion.9, f32[384,256]{1,0:T(8,128)S(1)} %convolution_subtract_fusion.10, ...), kind=kOutput, calls=%fused_computation.33 | convolution fusion | flops 3628596736 | bytes 14163968 | tf_op jit(solution)/shard_map/dot_general | solution.py:93
  299.5 3.8 collective-permute-start.20
  303.3 3.9 collective-permute-start.22
  310.6 139.0 %all-reduce.5.cloned.1.call-done = f32[520,256]{1,0:T(8,128)} async-done(((f32[520,256]{1,0:T(8,128)}), f32[520,256]{1,0:T(8,128)}) %all-reduce.5.cloned.1.call-update) | async-done | bytes 532496 | tf_op jit(solution)/shard_map/psum | solution.py:77
  450.4 3.9 fusion.40
  468.3 5.2 %fusion.29 = f32[1,1,1536,256]{3,2,1,0:T(8,128)} fusion(f32[1536,256]{1,0:T(8,128)S(1)} %copy-done.23, f32[384,256]{1,0:T(8,128)S(1)} %convolution_subtract_fusion.4, f32[384,256]{1,0:T(8,128)S(1)} %convolution_subtract_fusion.5, f32[384,256]{1,0:T(8,128)S(1)} %convolution_subtract_fusion.6, f32[384,256]{1,0:T(8,128)S(1)} %convolution_subtract_fusion.7, ...), kind=kOutput, calls=%fused_computation.31 | convolution fusion | flops 2422603776 | bytes 9963520 | tf_op jit(solution)/shard_map/dot_general | solution.py:82
  (197 shorter events, 93.1 us)
Async XLA Ops:
  7.2 108.1 %all-gather.3.cloned.1.call-start = ((), (), s32[]{:S(2)}) async-start(), calls=%async_computation.2 | async-start | bytes 1056768 | tf_op jit(solution)/shard_map/all_gather | solution.py:54
  7.9 243.1 %all-reduce.3.cloned.1.call-start = ((), (), s32[]{:S(2)}) async-start(), calls=%async_computation | async-start | bytes 1064960 | tf_op jit(solution)/shard_map/psum | solution.py:77
  9.5 36.9 %collective-permute-start.12 = (f32[392,16]{0,1:T(8,128)S(1)}, f32[392,16]{0,1:T(8,128)S(1)}, u32[]{:S(2)}, u32[]{:S(2)}) collective-permute-start(f32[392,16]{0,1:T(8,128)S(1)} %get-tuple-element.28), channel_id=1, source_target_pairs={{0,16},{16,32},{32,48},{48,64},{64,80},{80,96},{96,112},{1,17},{17... | collective-permute-start | bytes 75272 | tf_op jit(solution)/shard_map/ppermute | solution.py:13
  14.1 28.5 %collective-permute-start.13 = (f32[392,16]{0,1:T(8,128)S(1)}, f32[392,16]{0,1:T(8,128)S(1)}, u32[]{:S(2)}, u32[]{:S(2)}) collective-permute-start(f32[392,16]{0,1:T(8,128)S(1)} %get-tuple-element.29), channel_id=1, source_target_pairs={{16,0},{32,16},{48,32},{64,48},{80,64},{96,80},{112,96},{17,1},{33... | collective-permute-start | bytes 75272 | tf_op jit(solution)/shard_map/ppermute | solution.py:13
  16.0 20.4 %collective-permute-start.14 = (f32[392,16]{0,1:T(8,128)S(1)}, f32[392,16]{0,1:T(8,128)S(1)}, u32[]{:S(2)}, u32[]{:S(2)}) collective-permute-start(f32[392,16]{0,1:T(8,128)S(1)} %get-tuple-element.30), channel_id=1, source_target_pairs={{0,1},{1,2},{2,3},{3,4},{4,5},{5,6},{6,7},{7,8},{8,9},{9,10},{10,1... | collective-permute-start | bytes 75272 | tf_op jit(solution)/shard_map/ppermute | solution.py:13
  19.6 11.7 %collective-permute-start.15 = (f32[392,16]{0,1:T(8,128)S(1)}, f32[392,16]{0,1:T(8,128)S(1)}, u32[]{:S(2)}, u32[]{:S(2)}) collective-permute-start(f32[392,16]{0,1:T(8,128)S(1)} %get-tuple-element.31), channel_id=1, source_target_pairs={{1,0},{2,1},{3,2},{4,3},{5,4},{6,5},{7,6},{8,7},{9,8},{10,9},{11,1... | collective-permute-start | bytes 75272 | tf_op jit(solution)/shard_map/ppermute | solution.py:13
  23.5 23.4 %collective-permute-start = (f32[384,256]{1,0:T(8,128)}, f32[384,256]{1,0:T(8,128)}, u32[]{:S(2)}, u32[]{:S(2)}) collective-permute-start(f32[384,256]{1,0:T(8,128)} %get-tuple-element.20), channel_id=1, source_target_pairs={{0,16},{16,32},{32,48},{48,64},{64,80},{80,96},{96,112},{1,17},{17... | collective-permute-start | bytes 1179656 | tf_op jit(solution)/shard_map/ppermute | solution.py:13
  31.2 17.3 %collective-permute-start.1 = (f32[384,256]{1,0:T(8,128)}, f32[384,256]{1,0:T(8,128)S(1)}, u32[]{:S(2)}, u32[]{:S(2)}) collective-permute-start(f32[384,256]{1,0:T(8,128)} %get-tuple-element.21), channel_id=1, source_target_pairs={{16,0},{32,16},{48,32},{64,48},{80,64},{96,80},{112,96},{17,1},{33... | collective-permute-start | bytes 1179656 | tf_op jit(solution)/shard_map/ppermute | solution.py:13
  36.4 12.7 %collective-permute-start.2 = (f32[384,256]{1,0:T(8,128)}, f32[384,256]{1,0:T(8,128)S(1)}, u32[]{:S(2)}, u32[]{:S(2)}) collective-permute-start(f32[384,256]{1,0:T(8,128)} %get-tuple-element.22), channel_id=1, source_target_pairs={{0,1},{1,2},{2,3},{3,4},{4,5},{5,6},{6,7},{7,8},{8,9},{9,10},{10,1... | collective-permute-start | bytes 1179656 | tf_op jit(solution)/shard_map/ppermute | solution.py:13
  42.6 12.9 %collective-permute-start.3 = (f32[384,256]{1,0:T(8,128)S(1)}, f32[384,256]{1,0:T(8,128)S(1)}, u32[]{:S(2)}, u32[]{:S(2)}) collective-permute-start(f32[384,256]{1,0:T(8,128)S(1)} %copy-done.29), channel_id=1, source_target_pairs={{1,0},{2,1},{3,2},{4,3},{5,4},{6,5},{7,6},{8,7},{9,8},{10,9},{11,1... | collective-permute-start | bytes 1179656 | tf_op jit(solution)/shard_map/ppermute | solution.py:13
  60.4 13.2 %collective-permute-start.4 = (f32[384,256]{1,0:T(8,128)S(1)}, f32[384,256]{1,0:T(8,128)S(1)}, u32[]{:S(2)}, u32[]{:S(2)}) collective-permute-start(f32[384,256]{1,0:T(8,128)S(1)} %get-tuple-element.16), channel_id=1, source_target_pairs={{0,16},{16,32},{32,48},{48,64},{64,80},{80,96},{96,112},{1,17},{17... | collective-permute-start | bytes 1179656 | tf_op jit(solution)/shard_map/ppermute | solution.py:13
  66.4 11.9 %collective-permute-start.6 = (f32[384,256]{1,0:T(8,128)S(1)}, f32[384,256]{1,0:T(8,128)S(1)}, u32[]{:S(2)}, u32[]{:S(2)}) collective-permute-start(f32[384,256]{1,0:T(8,128)S(1)} %get-tuple-element.17), channel_id=1, source_target_pairs={{0,1},{1,2},{2,3},{3,4},{4,5},{5,6},{6,7},{7,8},{8,9},{9,10},{10,1... | collective-permute-start | bytes 1179656 | tf_op jit(solution)/shard_map/ppermute | solution.py:13
  69.8 12.4 %collective-permute-start.7 = (f32[384,256]{1,0:T(8,128)S(1)}, f32[384,256]{1,0:T(8,128)S(1)}, u32[]{:S(2)}, u32[]{:S(2)}) collective-permute-start(f32[384,256]{1,0:T(8,128)S(1)} %get-tuple-element.18), channel_id=1, source_target_pairs={{1,0},{2,1},{3,2},{4,3},{5,4},{6,5},{7,6},{8,7},{9,8},{10,9},{11,1... | collective-permute-start | bytes 1179656 | tf_op jit(solution)/shard_map/ppermute | solution.py:13
  71.1 11.6 %collective-permute-start.5 = (f32[384,256]{1,0:T(8,128)S(1)}, f32[384,256]{1,0:T(8,128)S(1)}, u32[]{:S(2)}, u32[]{:S(2)}) collective-permute-start(f32[384,256]{1,0:T(8,128)S(1)} %get-tuple-element.19), channel_id=1, source_target_pairs={{16,0},{32,16},{48,32},{64,48},{80,64},{96,80},{112,96},{17,1},{33... | collective-permute-start | bytes 1179656 | tf_op jit(solution)/shard_map/ppermute | solution.py:13
  88.4 15.0 %collective-permute-start.8 = (f32[384,256]{1,0:T(8,128)}, f32[384,256]{1,0:T(8,128)}, u32[]{:S(2)}, u32[]{:S(2)}) collective-permute-start(f32[384,256]{1,0:T(8,128)} %get-tuple-element.12), channel_id=1, source_target_pairs={{0,16},{16,32},{32,48},{48,64},{64,80},{80,96},{96,112},{1,17},{17... | collective-permute-start | bytes 1179656 | tf_op jit(solution)/shard_map/ppermute | solution.py:13
  92.5 13.6 %collective-permute-start.10 = (f32[384,256]{1,0:T(8,128)}, f32[384,256]{1,0:T(8,128)}, u32[]{:S(2)}, u32[]{:S(2)}) collective-permute-start(f32[384,256]{1,0:T(8,128)} %get-tuple-element.13), channel_id=1, source_target_pairs={{0,1},{1,2},{2,3},{3,4},{4,5},{5,6},{6,7},{7,8},{8,9},{9,10},{10,1... | collective-permute-start | bytes 1179656 | tf_op jit(solution)/shard_map/ppermute | solution.py:13
  98.1 12.5 %collective-permute-start.11 = (f32[384,256]{1,0:T(8,128)S(1)}, f32[384,256]{1,0:T(8,128)}, u32[]{:S(2)}, u32[]{:S(2)}) collective-permute-start(f32[384,256]{1,0:T(8,128)S(1)} %get-tuple-element.14), channel_id=1, source_target_pairs={{1,0},{2,1},{3,2},{4,3},{5,4},{6,5},{7,6},{8,7},{9,8},{10,9},{11,1... | collective-permute-start | bytes 1179656 | tf_op jit(solution)/shard_map/ppermute | solution.py:13
  99.4 13.6 %collective-permute-start.9 = (f32[384,256]{1,0:T(8,128)S(1)}, f32[384,256]{1,0:T(8,128)}, u32[]{:S(2)}, u32[]{:S(2)}) collective-permute-start(f32[384,256]{1,0:T(8,128)S(1)} %get-tuple-element.15), channel_id=1, source_target_pairs={{16,0},{32,16},{48,32},{64,48},{80,64},{96,80},{112,96},{17,1},{33... | collective-permute-start | bytes 1179656 | tf_op jit(solution)/shard_map/ppermute | solution.py:13
  103.2 346.4 %all-reduce.5.cloned.1.call-start = ((), (), s32[]{:S(2)}) async-start(), calls=%async_computation.1 | async-start | bytes 1064960 | tf_op jit(solution)/shard_map/psum | solution.py:77
  277.3 12.2 %collective-permute-start.19 = (f32[384,256]{1,0:T(8,128)S(1)}, f32[384,256]{1,0:T(8,128)S(1)}, u32[]{:S(2)}, u32[]{:S(2)}) collective-permute-start(f32[384,256]{1,0:T(8,128)S(1)} %get-tuple-element.10), channel_id=1, source_target_pairs={{1,0},{2,1},{3,2},{4,3},{5,4},{6,5},{7,6},{8,7},{9,8},{10,9},{11,1... | collective-permute-start | bytes 1179656 | tf_op jit(solution)/shard_map/ppermute | solution.py:13
  299.5 162.1 %collective-permute-start.20 = (f32[384,256]{1,0:T(8,128)}, f32[384,256]{1,0:T(8,128)}, u32[]{:S(2)}, u32[]{:S(2)}) collective-permute-start(f32[384,256]{1,0:T(8,128)} %get-tuple-element.4), channel_id=1, source_target_pairs={{0,16},{16,32},{32,48},{48,64},{64,80},{80,96},{96,112},{1,17},{17... | collective-permute-start | bytes 1179656 | tf_op jit(solution)/shard_map/ppermute | solution.py:13
  303.3 160.0 %collective-permute-start.22 = (f32[384,256]{1,0:T(8,128)}, f32[384,256]{1,0:T(8,128)}, u32[]{:S(2)}, u32[]{:S(2)}) collective-permute-start(f32[384,256]{1,0:T(8,128)} %get-tuple-element.5), channel_id=1, source_target_pairs={{0,1},{1,2},{2,3},{3,4},{4,5},{5,6},{6,7},{7,8},{8,9},{9,10},{10,1... | collective-permute-start | bytes 1179656 | tf_op jit(solution)/shard_map/ppermute | solution.py:13
  307.2 157.8 %collective-permute-start.23 = (f32[384,256]{1,0:T(8,128)}, f32[384,256]{1,0:T(8,128)}, u32[]{:S(2)}, u32[]{:S(2)}) collective-permute-start(f32[384,256]{1,0:T(8,128)} %get-tuple-element.6), channel_id=1, source_target_pairs={{1,0},{2,1},{3,2},{4,3},{5,4},{6,5},{7,6},{8,7},{9,8},{10,9},{11,1... | collective-permute-start | bytes 1179656 | tf_op jit(solution)/shard_map/ppermute | solution.py:13
  308.4 158.2 %collective-permute-start.21 = (f32[384,256]{1,0:T(8,128)}, f32[384,256]{1,0:T(8,128)}, u32[]{:S(2)}, u32[]{:S(2)}) collective-permute-start(f32[384,256]{1,0:T(8,128)} %get-tuple-element.7), channel_id=1, source_target_pairs={{16,0},{32,16},{48,32},{64,48},{80,64},{96,80},{112,96},{17,1},{33... | collective-permute-start | bytes 1179656 | tf_op jit(solution)/shard_map/ppermute | solution.py:13
  (45 other events, 484.8 us)
Sparse Core Ops, SparseCore 0:
  10.8 72.5 all-gather.2
  103.3 147.5 all-reduce.2
  298.4 151.1 all-reduce.4
where the time goes:
time: 486 us; the launch traced here: 480 us
  waiting for transfers between devices  297 us (61%)
  matrix products  78.2 us (16%)
  starting transfers between devices  68.4 us (14%)
  between operations  15.1 us (3%)
  local copies, waits for them, and re-layouts  12.4 us (3%)
  other arithmetic  9.11 us (2%)
    psum x2, waiting for transfers between devices, reduced(): total = lax.psum(jnp.dot(place, block, precision=HIGHEST), ('sx', 'sy'))  273 us
    ppermute x24, starting transfers between devices, shifted(): return lax.ppermute(block, axis, route)  68.1 us
    ppermute x24, waiting for transfers between devices, shifted(): return lax.ppermute(block, axis, route)  23.2 us
    dot_general x20, matrix products, jump(): jnp.dot(match[f], received[f], precision=HIGHEST)  23.1 us
    dot_general x2, matrix products, precondition(): applied = jnp.dot(prec_mat, spread, precision=HIGH)  11.6 us
    dot_general x2, matrix products, coarse(): return (jnp.dot(coupling_jump, sol, precision=HIGHEST), inner(rhs, sol))  10.9 us
    dot_general x2, matrix products, flexible(): jnp.dot(flex_mat, spread, precision=HIGH)  9.93 us
  transfers between devices with their start and end apart: 27, of which 9 were waited for; matrix products, arithmetic and copies ran while one was open for 13% of the time, Pallas kernels for 0%

commit v1 on v0

--- a/solution.py
+++ b/solution.py
@@ -74,7 +74,8 @@
     def reduced(local_load, *rows):
         rows = list(rows) + [jnp.zeros_like(rows[0])] * (3 - len(rows))
         block = jnp.concatenate([local_load] + [row[None] for row in rows], axis=0)
-        total = lax.psum(jnp.dot(place, block, precision=HIGHEST), ("sx", "sy"))
+        half = lax.psum(jnp.dot(place, block, precision=HIGHEST), "sx")
+        total = lax.psum(half, "sy")
         return (total[:ncoarse], total[ncoarse + 1], total[ncoarse + 2], total[ncoarse + 3])
 
     def coarse(rhs):

time: 486 us -> 452 us (0.930)
  waiting for transfers between devices: 297 us -> 257 us
  matrix products: 78.2 us -> 85.5 us
    psum x2 -> x4, waiting for transfers between devices: 273 us -> 228 us  [the longest x2 149 us: reduced(): total = lax.psum(half, 'sy')]
    all_gather x1, waiting for transfers between devices: 0.01 us -> 7.75 us  [shards(): inverse = lax.all_gather(coarse_inverse, ('sx', 'sy'), axis=0, tiled=True)]
    dot_general x20, matrix products: 23.1 us -> 29 us  [jump(): jnp.dot(match[f], received[f], precision=HIGHEST)]
  transfers between devices with their start and end apart: 27 -> 29, of which waited for: 9 -> 12; matrix products, arithmetic and copies ran while one was open for 13% -> 9% of each run, Pallas kernels for 0% -> 0%
where the time goes in v1:
time: 452 us; the launch traced here: 444 us
  waiting for transfers between devices  257 us (57%)
  matrix products  85.5 us (19%)
  starting transfers between devices  68.1 us (15%)
  between operations  16.6 us (4%)
  local copies, waits for them, and re-layouts  9.63 us (2%)
  other arithmetic  6.94 us (2%)
    psum x2, waiting for transfers between devices, reduced(): total = lax.psum(half, 'sy')  149 us
    psum x2, waiting for transfers between devices, reduced(): half = lax.psum(jnp.dot(place, block, precision=HIGHEST), 'sx')  78.6 us
    ppermute x24, starting transfers between devices, shifted(): return lax.ppermute(block, axis, route)  67.9 us
    dot_general x20, matrix products, jump(): jnp.dot(match[f], received[f], precision=HIGHEST)  29 us
    ppermute x24, waiting for transfers between devices, shifted(): return lax.ppermute(block, axis, route)  21.5 us
    dot_general x2, matrix products, precondition(): applied = jnp.dot(prec_mat, spread, precision=HIGH)  15.4 us
    dot_general x2, matrix products, coarse(): return (jnp.dot(coupling_jump, sol, precision=HIGHEST), inner(rhs, sol))  12.3 us
  transfers between devices with their start and end apart: 29, of which 12 were waited for; matrix products, arithmetic and copies ran while one was open for 9% of the time, Pallas kernels for 0%

profile of v1, /device:TPU:1, one launch (start us, length us, event | category | flops | bytes accessed | tf_op | source)
XLA Modules:
  0.0 443.7 jit_solution(15542945541701174909)
XLA Ops:
  10.6 4.6 %collective-permute-start = (f32[384,256]{1,0:T(8,128)}, f32[384,256]{1,0:T(8,128)}, u32[]{:S(2)}, u32[]{:S(2)}) collective-permute-start(f32[384,256]{1,0:T(8,128)} %get-tuple-element.20), channel_id=1, source_target_pairs={{0,16},{16,32},{32,48},{48,64},{64,80},{80,96},{96,112},{1,17},{17... | collective-permute-start | bytes 1179656 | tf_op jit(solution)/shard_map/ppermute | solution.py:13
  17.1 4.3 collective-permute-start.2
  35.4 8.0 %multiply_reduce_fusion.4 = (f32[256]{0:T(256)S(1)}, f32[1536,256]{1,0:T(8,128)S(1)}) fusion(f32[1536]{0:T(1024)S(1)} %mul.194, f32[384,256]{1,0:T(8,128)S(1)} %convolution_subtract_fusion.20, f32[384,256]{1,0:T(8,128)S(1)} %convolution_subtract_fusion.21, f32[384,256]{1,0:T(8,128)S(1)} %convolution_subtract_fusion.22, ...), kind=kOutput, calls=%fused_computation.36 | convolution fusion | flops 3627810560 | bytes 12590080 | tf_op jit(solution)/shard_map/dot_general | solution.py:87
  43.5 4.4 collective-permute-start.4
  58.8 3.6 collective-permute-done.7
  64.2 4.1 multiply_reduce_fusion.3
  69.7 4.3 collective-permute-start.12
  91.7 4.4 %collective-permute-start.8 = (f32[384,256]{1,0:T(8,128)}, f32[384,256]{1,0:T(8,128)}, u32[]{:S(2)}, u32[]{:S(2)}) collective-permute-start(f32[384,256]{1,0:T(8,128)} %get-tuple-element.12), channel_id=1, source_target_pairs={{0,16},{16,32},{32,48},{48,64},{64,80},{80,96},{96,112},{1,17},{17... | collective-permute-start | bytes 1179656 | tf_op jit(solution)/shard_map/ppermute | solution.py:13
  96.7 4.6 %collective-permute-start.10 = (f32[384,256]{1,0:T(8,128)}, f32[384,256]{1,0:T(8,128)}, u32[]{:S(2)}, u32[]{:S(2)}) collective-permute-start(f32[384,256]{1,0:T(8,128)} %get-tuple-element.13), channel_id=1, source_target_pairs={{0,1},{1,2},{2,3},{3,4},{4,5},{5,6},{6,7},{7,8},{8,9},{9,10},{10,1... | collective-permute-start | bytes 1179656 | tf_op jit(solution)/shard_map/ppermute | solution.py:13
  105.9 25.8 %all-reduce.5.cloned.1.call-done = f32[520,256]{1,0:T(8,128)} async-done(((f32[520,256]{1,0:T(8,128)}), f32[520,256]{1,0:T(8,128)}) %all-reduce.5.cloned.1.call-update) | async-done | bytes 532496 | tf_op jit(solution)/shard_map/psum | solution.py:77
  141.0 7.7 %all-gather.3.cloned.1.call-done = f32[128,4,512]{2,1,0:T(4,128)} async-done(((f32[1,4,512]{2,1,0:T(4,128)}), f32[128,4,512]{2,1,0:T(4,128)}) %all-gather.3.cloned.1.call-update) | async-done | bytes 1048592 | tf_op jit(solution)/shard_map/all_gather | solution.py:54
  150.4 69.9 %all-reduce.7.cloned.1.call-done = f32[520,256]{1,0:T(8,128)} async-done(((f32[520,256]{1,0:T(8,128)}), f32[520,256]{1,0:T(8,128)}) %all-reduce.7.cloned.1.call-update) | async-done | bytes 532496 | tf_op jit(solution)/shard_map/psum | solution.py:78
  220.2 3.7 fusion.36
  228.0 5.7 %fusion.9 = f32[1536,256]{1,0:T(8,128)S(1)} fusion(f32[256,512]{1,0:T(8,128)} %fusion.36, f32[384,512]{1,0:T(8,128)} %convolution_subtract_fusion, f32[384,512]{1,0:T(8,128)} %convolution_subtract_fusion.1, f32[384,512]{1,0:T(8,128)} %convolution_subtract_fusion.2, f32[384,512]{1,0:T(8,128)} %convolution_subtract_fusion.3, ...), kind=kOutput, calls=%fused_computation.11 | convolution fusion | flops 2421817344 | bytes 8389632 | tf_op jit(solution)/shard_map/dot_general | solution.py:83
  233.8 7.4 %multiply_reduce_fusion.2 = (f32[256]{0:T(256)S(1)}, f32[1536,256]{1,0:T(8,128)S(1)}) fusion(f32[1536,256]{1,0:T(8,128)S(1)} %fusion.9, f32[1536]{0:T(1024)S(1)} %mul.194, f32[1,1,1536,1536]{3,2,1,0:T(8,128)} %param.9), kind=kOutput, calls=%fused_computation.34 | convolution fusion | flops 3625451264 | bytes 12590080 | tf_op jit(solution)/shard_map/dot_general | solution.py:87
  241.4 5.2 %collective-permute-start.16 = (f32[384,256]{1,0:T(8,128)S(1)}, f32[384,256]{1,0:T(8,128)S(1)}, u32[]{:S(2)}, u32[]{:S(2)}) collective-permute-start(f32[384,256]{1,0:T(8,128)S(1)} %get-tuple-element.8), channel_id=1, source_target_pairs={{0,16},{16,32},{32,48},{48,64},{64,80},{80,96},{96,112},{1,17},{17... | collective-permute-start | bytes 1179656 | tf_op jit(solution)/shard_map/ppermute | solution.py:13
  252.6 3.7 collective-permute-done.18
  256.8 3.6 collective-permute-done.19
  261.5 4.8 %multiply_reduce_fusion.1 = (f32[256]{0:T(256)S(1)}, f32[256]{0:T(256)S(1)}, f32[1536,256]{1,0:T(8,128)S(1)}) fusion(f32[1536]{0:T(1024)S(1)} %broadcast_multiply_fusion, f32[384,256]{1,0:T(8,128)S(1)} %convolution_subtract_fusion.8, f32[384,256]{1,0:T(8,128)S(1)} %convolution_subtract_fusion.9, f32[384,256]{1,0:T(8,128)S(1)} %convolution_subtract_fusion.10, ...), kind=kOutput, calls=%fused_computation.33 | convolution fusion | flops 3628596736 | bytes 14163968 | tf_op jit(solution)/shard_map/dot_general | solution.py:94
  268.2 4.1 collective-permute-start.20
  273.5 3.6 collective-permute-start.22
  280.7 52.8 %all-reduce.9.cloned.1.call-done = f32[520,256]{1,0:T(8,128)} async-done(((f32[520,256]{1,0:T(8,128)}), f32[520,256]{1,0:T(8,128)}) %all-reduce.9.cloned.1.call-update) | async-done | bytes 532496 | tf_op jit(solution)/shard_map/psum | solution.py:77
  342.8 79.1 %all-reduce.11.cloned.1.call-done = f32[520,256]{1,0:T(8,128)} async-done(((f32[520,256]{1,0:T(8,128)}), f32[520,256]{1,0:T(8,128)}) %all-reduce.11.cloned.1.call-update) | async-done | bytes 532496 | tf_op jit(solution)/shard_map/psum | solution.py:78
  428.2 6.6 %fusion.29 = f32[1,1,1536,256]{3,2,1,0:T(8,128)} fusion(f32[1536,256]{1,0:T(8,128)S(1)} %copy-done.25, f32[384,256]{1,0:T(8,128)} %convolution_subtract_fusion.4, f32[384,256]{1,0:T(8,128)} %convolution_subtract_fusion.5, f32[384,256]{1,0:T(8,128)} %convolution_subtract_fusion.6, f32[384,256]{1,0:T(8,128)} %convolution_subtract_fusion.7, ...), kind=kOutput, calls=%fused_computation.31 | convolution fusion | flops 2422603776 | bytes 9963520 | tf_op jit(solution)/shard_map/dot_general | solution.py:83
  (191 shorter events, 101.1 us)
Async XLA Ops:
  8.0 123.6 %all-reduce.5.cloned.1.call-start = ((), (), s32[]{:S(2)}) async-start(), calls=%async_computation | async-start | bytes 1064960 | tf_op jit(solution)/shard_map/psum | solution.py:77
  10.6 12.9 %collective-permute-start = (f32[384,256]{1,0:T(8,128)}, f32[384,256]{1,0:T(8,128)}, u32[]{:S(2)}, u32[]{:S(2)}) collective-permute-start(f32[384,256]{1,0:T(8,128)} %get-tuple-element.20), channel_id=1, source_target_pairs={{0,16},{16,32},{32,48},{48,64},{64,80},{80,96},{96,112},{1,17},{17... | collective-permute-start | bytes 1179656 | tf_op jit(solution)/shard_map/ppermute | solution.py:13
  17.1 11.7 %collective-permute-start.2 = (f32[384,256]{1,0:T(8,128)S(1)}, f32[384,256]{1,0:T(8,128)}, u32[]{:S(2)}, u32[]{:S(2)}) collective-permute-start(f32[384,256]{1,0:T(8,128)S(1)} %get-tuple-element.22), channel_id=1, source_target_pairs={{0,1},{1,2},{2,3},{3,4},{4,5},{5,6},{6,7},{7,8},{8,9},{9,10},{10,1... | collective-permute-start | bytes 1179656 | tf_op jit(solution)/shard_map/ppermute | solution.py:13
  21.4 12.3 %collective-permute-start.3 = (f32[384,256]{1,0:T(8,128)S(1)}, f32[384,256]{1,0:T(8,128)}, u32[]{:S(2)}, u32[]{:S(2)}) collective-permute-start(f32[384,256]{1,0:T(8,128)S(1)} %get-tuple-element.23), channel_id=1, source_target_pairs={{1,0},{2,1},{3,2},{4,3},{5,4},{6,5},{7,6},{8,7},{9,8},{10,9},{11,1... | collective-permute-start | bytes 1179656 | tf_op jit(solution)/shard_map/ppermute | solution.py:13
  43.5 11.0 %collective-permute-start.4 = (f32[384,256]{1,0:T(8,128)S(1)}, f32[384,256]{1,0:T(8,128)S(1)}, u32[]{:S(2)}, u32[]{:S(2)}) collective-permute-start(f32[384,256]{1,0:T(8,128)S(1)} %get-tuple-element.16), channel_id=1, source_target_pairs={{0,16},{16,32},{32,48},{48,64},{64,80},{80,96},{96,112},{1,17},{17... | collective-permute-start | bytes 1179656 | tf_op jit(solution)/shard_map/ppermute | solution.py:13
  50.7 11.7 %collective-permute-start.7 = (f32[384,256]{1,0:T(8,128)S(1)}, f32[384,256]{1,0:T(8,128)S(1)}, u32[]{:S(2)}, u32[]{:S(2)}) collective-permute-start(f32[384,256]{1,0:T(8,128)S(1)} %get-tuple-element.18), channel_id=1, source_target_pairs={{1,0},{2,1},{3,2},{4,3},{5,4},{6,5},{7,6},{8,7},{9,8},{10,9},{11,1... | collective-permute-start | bytes 1179656 | tf_op jit(solution)/shard_map/ppermute | solution.py:13
  52.0 10.9 %collective-permute-start.5 = (f32[384,256]{1,0:T(8,128)S(1)}, f32[384,256]{1,0:T(8,128)S(1)}, u32[]{:S(2)}, u32[]{:S(2)}) collective-permute-start(f32[384,256]{1,0:T(8,128)S(1)} %get-tuple-element.19), channel_id=1, source_target_pairs={{16,0},{32,16},{48,32},{64,48},{80,64},{96,80},{112,96},{17,1},{33... | collective-permute-start | bytes 1179656 | tf_op jit(solution)/shard_map/ppermute | solution.py:13
  69.6 79.2 %all-gather.3.cloned.1.call-start = ((), (), s32[]{:S(2)}) async-start(), calls=%async_computation.4 | async-start | bytes 1056768 | tf_op jit(solution)/shard_map/all_gather | solution.py:54
  69.7 26.5 %collective-permute-start.12 = (f32[392,16]{0,1:T(8,128)S(1)}, f32[392,16]{0,1:T(8,128)S(1)}, u32[]{:S(2)}, u32[]{:S(2)}) collective-permute-start(f32[392,16]{0,1:T(8,128)S(1)} %get-tuple-element.28), channel_id=1, source_target_pairs={{0,16},{16,32},{32,48},{48,64},{64,80},{80,96},{96,112},{1,17},{17... | collective-permute-start | bytes 75272 | tf_op jit(solution)/shard_map/ppermute | solution.py:13
  74.0 11.4 %collective-permute-start.13 = (f32[392,16]{0,1:T(8,128)S(1)}, f32[392,16]{0,1:T(8,128)S(1)}, u32[]{:S(2)}, u32[]{:S(2)}) collective-permute-start(f32[392,16]{0,1:T(8,128)S(1)} %get-tuple-element.29), channel_id=1, source_target_pairs={{16,0},{32,16},{48,32},{64,48},{80,64},{96,80},{112,96},{17,1},{33... | collective-permute-start | bytes 75272 | tf_op jit(solution)/shard_map/ppermute | solution.py:13
  80.7 139.5 %all-reduce.7.cloned.1.call-start = ((), (), s32[]{:S(2)}) async-start(), calls=%async_computation.1 | async-start | bytes 1064960 | tf_op jit(solution)/shard_map/psum | solution.py:78
  91.7 40.0 %collective-permute-start.8 = (f32[384,256]{1,0:T(8,128)}, f32[384,256]{1,0:T(8,128)}, u32[]{:S(2)}, u32[]{:S(2)}) collective-permute-start(f32[384,256]{1,0:T(8,128)} %get-tuple-element.12), channel_id=1, source_target_pairs={{0,16},{16,32},{32,48},{48,64},{64,80},{80,96},{96,112},{1,17},{17... | collective-permute-start | bytes 1179656 | tf_op jit(solution)/shard_map/ppermute | solution.py:13
  96.7 37.4 %collective-permute-start.10 = (f32[384,256]{1,0:T(8,128)}, f32[384,256]{1,0:T(8,128)}, u32[]{:S(2)}, u32[]{:S(2)}) collective-permute-start(f32[384,256]{1,0:T(8,128)} %get-tuple-element.13), channel_id=1, source_target_pairs={{0,1},{1,2},{2,3},{3,4},{4,5},{5,6},{6,7},{7,8},{8,9},{9,10},{10,1... | collective-permute-start | bytes 1179656 | tf_op jit(solution)/shard_map/ppermute | solution.py:13
  102.7 33.7 %collective-permute-start.11 = (f32[384,256]{1,0:T(8,128)S(1)}, f32[384,256]{1,0:T(8,128)}, u32[]{:S(2)}, u32[]{:S(2)}) collective-permute-start(f32[384,256]{1,0:T(8,128)S(1)} %get-tuple-element.14), channel_id=1, source_target_pairs={{1,0},{2,1},{3,2},{4,3},{5,4},{6,5},{7,6},{8,7},{9,8},{10,9},{11,1... | collective-permute-start | bytes 1179656 | tf_op jit(solution)/shard_map/ppermute | solution.py:13
  104.0 34.7 %collective-permute-start.9 = (f32[384,256]{1,0:T(8,128)S(1)}, f32[384,256]{1,0:T(8,128)}, u32[]{:S(2)}, u32[]{:S(2)}) collective-permute-start(f32[384,256]{1,0:T(8,128)S(1)} %get-tuple-element.15), channel_id=1, source_target_pairs={{16,0},{32,16},{48,32},{64,48},{80,64},{96,80},{112,96},{17,1},{33... | collective-permute-start | bytes 1179656 | tf_op jit(solution)/shard_map/ppermute | solution.py:13
  131.7 201.8 %all-reduce.9.cloned.1.call-start = ((), (), s32[]{:S(2)}) async-start(), calls=%async_computation.2 | async-start | bytes 1064960 | tf_op jit(solution)/shard_map/psum | solution.py:77
  241.4 10.6 %collective-permute-start.16 = (f32[384,256]{1,0:T(8,128)S(1)}, f32[384,256]{1,0:T(8,128)S(1)}, u32[]{:S(2)}, u32[]{:S(2)}) collective-permute-start(f32[384,256]{1,0:T(8,128)S(1)} %get-tuple-element.8), channel_id=1, source_target_pairs={{0,16},{16,32},{32,48},{48,64},{64,80},{80,96},{96,112},{1,17},{17... | collective-permute-start | bytes 1179656 | tf_op jit(solution)/shard_map/ppermute | solution.py:13
  248.6 11.8 %collective-permute-start.19 = (f32[384,256]{1,0:T(8,128)S(1)}, f32[384,256]{1,0:T(8,128)S(1)}, u32[]{:S(2)}, u32[]{:S(2)}) collective-permute-start(f32[384,256]{1,0:T(8,128)S(1)} %get-tuple-element.10), channel_id=1, source_target_pairs={{1,0},{2,1},{3,2},{4,3},{5,4},{6,5},{7,6},{8,7},{9,8},{10,9},{11,1... | collective-permute-start | bytes 1179656 | tf_op jit(solution)/shard_map/ppermute | solution.py:13
  249.9 11.0 %collective-permute-start.17 = (f32[384,256]{1,0:T(8,128)S(1)}, f32[384,256]{1,0:T(8,128)S(1)}, u32[]{:S(2)}, u32[]{:S(2)}) collective-permute-start(f32[384,256]{1,0:T(8,128)S(1)} %get-tuple-element.11), channel_id=1, source_target_pairs={{16,0},{32,16},{48,32},{64,48},{80,64},{96,80},{112,96},{17,1},{33... | collective-permute-start | bytes 1179656 | tf_op jit(solution)/shard_map/ppermute | solution.py:13
  268.2 65.3 %collective-permute-start.20 = (f32[384,256]{1,0:T(8,128)}, f32[384,256]{1,0:T(8,128)}, u32[]{:S(2)}, u32[]{:S(2)}) collective-permute-start(f32[384,256]{1,0:T(8,128)} %get-tuple-element.4), channel_id=1, source_target_pairs={{0,16},{16,32},{32,48},{48,64},{64,80},{80,96},{96,112},{1,17},{17... | collective-permute-start | bytes 1179656 | tf_op jit(solution)/shard_map/ppermute | solution.py:13
  273.5 148.3 %all-reduce.11.cloned.1.call-start = ((), (), s32[]{:S(2)}) async-start(), calls=%async_computation.3 | async-start | bytes 1064960 | tf_op jit(solution)/shard_map/psum | solution.py:78
  273.5 62.3 %collective-permute-start.22 = (f32[384,256]{1,0:T(8,128)}, f32[384,256]{1,0:T(8,128)}, u32[]{:S(2)}, u32[]{:S(2)}) collective-permute-start(f32[384,256]{1,0:T(8,128)} %get-tuple-element.5), channel_id=1, source_target_pairs={{0,1},{1,2},{2,3},{3,4},{4,5},{5,6},{6,7},{7,8},{8,9},{9,10},{10,1... | collective-permute-start | bytes 1179656 | tf_op jit(solution)/shard_map/ppermute | solution.py:13
  277.2 61.0 %collective-permute-start.23 = (f32[384,256]{1,0:T(8,128)}, f32[384,256]{1,0:T(8,128)}, u32[]{:S(2)}, u32[]{:S(2)}) collective-permute-start(f32[384,256]{1,0:T(8,128)} %get-tuple-element.6), channel_id=1, source_target_pairs={{1,0},{2,1},{3,2},{4,3},{5,4},{6,5},{7,6},{8,7},{9,8},{10,9},{11,1... | collective-permute-start | bytes 1179656 | tf_op jit(solution)/shard_map/ppermute | solution.py:13
  278.5 62.0 %collective-permute-start.21 = (f32[384,256]{1,0:T(8,128)}, f32[384,256]{1,0:T(8,128)}, u32[]{:S(2)}, u32[]{:S(2)}) collective-permute-start(f32[384,256]{1,0:T(8,128)} %get-tuple-element.7), channel_id=1, source_target_pairs={{16,0},{32,16},{48,32},{64,48},{80,64},{96,80},{112,96},{17,1},{33... | collective-permute-start | bytes 1179656 | tf_op jit(solution)/shard_map/ppermute | solution.py:13
  (41 other events, 497.2 us)
Sparse Core Ops, SparseCore 0:
  69.7 61.9 all-reduce.4
  135.0 85.2 all-reduce.6
  273.6 59.8 all-reduce.8
  336.6 85.1 all-reduce.10
Sparse Core Ops, SparseCore 1:
  80.8 67.9 all-gather.2
